TPU v7x, 128 devices: a whole 4x4x4 slice. The times are simulated.
128 devices in a mesh: expert: 32 (over y, z, core), vocab: 4 (over x).
Axes of the slice: x: 4, y: 4, z: 4, core: 2. Of those that a mesh axis runs over, the one named last changes fastest.
Arguments:
- tokens: bfloat16 [4096, 2048], P('expert'), may hold values from -12 to 12
- expert_ids: int32 [4096, 6], P('expert'), may hold values from 0 to 63, all different within a row; in each aligned block of 128 rows (0 to 127, 128 to 255, ...) at most 24 rows name the same one
- gates: float32 [4096, 6], P('expert'), may hold values from 0.05 to 0.4
- w_gate: bfloat16 [64, 2048, 1408], P('expert', None, 'vocab'), may hold values from -0.125 to 0.125
- w_up: bfloat16 [64, 2048, 1408], P('expert', None, 'vocab'), may hold values from -0.125 to 0.125
- w_down: bfloat16 [64, 1408, 2048], P('expert', 'vocab'), may hold values from -0.21875 to 0.21875
- norm_gain: float32 [2048], replicated, may hold values from 0.5 to 1.5
- lm_weight: bfloat16 [2048, 98304], P(None, ('expert', 'vocab')), may hold values from -6.9605824 to 6.9605824
- targets: int32 [4096], P('expert'), may hold values from 0 to 98303
Outputs:
- logprobs: float32 [4096], P('expert')
Inputs may be any that keep to these rules, and one draw needn't show every extreme that they name: `expert_ids`: in the 128 rows of one device no expert is named by more than 24 routes; each row names 6 different experts.
All inputs are finite; a program needn't handle non-finite values.
Results may differ from a plain program's by a relative error of at most 0.003.
Values may be sent and summed in bfloat16 or wider, within the bound.
A program may use at most 128 MiB of HBM per device.

v0:
```python
import jax
import jax.numpy as jnp
from jax import lax
from jax.sharding import PartitionSpec as P


def split_up(array, dim, count):
    before, after = (array.shape[:dim], array.shape[dim + 1 :])
    return jnp.moveaxis(array.reshape(*before, count, -1, *after), dim, 0)


def piece_ends(length, count):
    unit = 8 if length >= 8 * count else 1
    return [length // unit * k // count * unit for k in range(1, count)]


def laid_out(parts, dim):
    shape = list(parts.shape[1:])
    shape[dim] *= parts.shape[0]
    return jnp.moveaxis(parts, 0, dim).reshape(shape)


def several_exchanges(array, axis, pieces, split_dim, concat_dim):
    parts = split_up(array, split_dim, lax.axis_size(axis))
    widest = max(range(1, max(2, parts.ndim - 1)), key=lambda d: parts.shape[d])
    done = []
    for share in jnp.split(parts, piece_ends(parts.shape[widest], pieces), axis=widest):
        if share.size:
            done.append(lax.all_to_all(share, axis, split_axis=0, concat_axis=0, tiled=True))
    return laid_out(jnp.concatenate(done, axis=widest), concat_dim)


def copy_for_each(array, axis):
    count = lax.axis_size(axis)
    return lax.all_to_all(
        jnp.broadcast_to(array[None], (count, *array.shape)), axis, 0, 0, tiled=True
    )


def taken_together(array, axis):
    everything = copy_for_each(array, axis)
    return jnp.sum(everything, axis=0)


def gathered_once(array, axis):
    leaves = jax.tree.leaves(array)
    turns = sorted(range(len(leaves)), key=lambda k: -leaves[k].size)
    width = (1, *leaves[turns[0]].shape)[-1]
    lines = [
        jnp.pad(leaves[k].reshape(-1), (0, -leaves[k].size % width)).reshape(-1, width)
        for k in turns
    ]
    both, at, found = (copy_for_each(jnp.concatenate(lines), axis), 0, {})
    for k, line in zip(turns, lines):
        share = both[:, at : at + len(line)].reshape(len(both), -1)
        found[k] = share[:, : leaves[k].size].reshape(-1, *leaves[k].shape)
        at += len(line)
    numbers = iter(range(len(leaves)))
    return jax.tree.map(lambda _: found[next(numbers)], array)


def joined_by_halves(pieces, combine):
    while len(jax.tree.leaves(pieces)[0]) > 1:
        pieces = jax.vmap(combine)(
            *(jax.tree.map(lambda part: part[side::2], pieces) for side in (0, 1))
        )
    return jax.tree.map(lambda part: part[0], pieces)


def joined_all(array, axis, combine):
    pieces = gathered_once(array, axis)
    return joined_by_halves(pieces, combine)


def expert_rows(received, w_gate, w_up, w_down):
    groups = w_gate.shape[0]
    shaped = received.reshape(-1, groups, received.shape[1], received.shape[2])
    gate_val = jnp.einsum("sltd,ldf->sltf", shaped, w_gate, preferred_element_type=jnp.float32)
    up_val = jnp.einsum("sltd,ldf->sltf", shaped, w_up, preferred_element_type=jnp.float32)
    hidden = (jax.nn.silu(gate_val) * up_val).astype(jnp.bfloat16)
    result = jnp.einsum("sltf,lfd->sltd", hidden, w_down, preferred_element_type=jnp.float32)
    return result.reshape(received.shape[0], received.shape[1], result.shape[3])


def shard_stats(logits, row_targets, base):
    columns = base + jnp.arange(logits.shape[1], dtype=jnp.int32)
    top_now = jnp.max(logits, axis=1)
    total_now = jnp.sum(jnp.exp(logits - top_now[:, None]), axis=1)
    picked_now = jnp.sum(jnp.where(columns[None, :] == row_targets[:, None], logits, 0.0), axis=1)
    return (top_now, total_now, picked_now)


def join_stats(first, second):
    best = jnp.maximum(first[0], second[0])
    mass = first[1] * jnp.exp(first[0] - best) + second[1] * jnp.exp(second[0] - best)
    return (best, mass, first[2] + second[2])


def body(tokens, expert_ids, gates, w_gate, w_up, w_down, norm_gain, lm_weight, targets):
    tok_rows = tokens.shape[0]
    top_count = expert_ids.shape[1]
    groups = w_gate.shape[0]
    width = tokens.shape[1]
    expert_devs = lax.axis_size("expert")
    vocab_devs = lax.axis_size("vocab")
    experts_all = groups * expert_devs
    slots = 2 * tok_rows * top_count // experts_all
    vocab_index = lax.axis_index("vocab")
    flat_ids = expert_ids.reshape(-1)
    onehot = (flat_ids[:, None] == jnp.arange(experts_all, dtype=jnp.int32)[None, :]).astype(
        jnp.int32
    )
    slot_ids = jnp.sum((jnp.cumsum(onehot, axis=0) - onehot) * onehot, axis=1)
    target_rows = (flat_ids * slots + slot_ids).reshape(tok_rows, top_count)
    places = jnp.arange(experts_all * slots, dtype=jnp.int32)
    packed = jnp.dot(
        jnp.any(places[:, None, None] == target_rows[None, :, :], axis=2).astype(jnp.bfloat16),
        tokens,
        preferred_element_type=jnp.float32,
    ).astype(jnp.bfloat16)
    packed = packed.reshape(experts_all, slots, width)
    partial_value = expert_rows(
        lax.all_to_all(packed, "expert", split_axis=0, concat_axis=0, tiled=True),
        w_gate,
        w_up,
        w_down,
    )
    combined = several_exchanges(partial_value, "expert", 2, 0, 0)
    flat_back = combined.reshape(experts_all * slots, combined.shape[2])
    picked = jnp.take(flat_back, target_rows.reshape(-1), axis=0).reshape(
        tok_rows, top_count, flat_back.shape[1]
    )
    mixture = jnp.sum(picked * gates[:, :, None], axis=1)
    base = (lax.axis_index("expert") * vocab_devs + vocab_index) * lm_weight.shape[1]
    mixture = taken_together(mixture, "vocab")
    resid = (tokens.astype(jnp.float32) + mixture).astype(jnp.bfloat16)
    resid_f = resid.astype(jnp.float32)
    squares = jnp.mean(resid_f * resid_f, axis=1)
    normed = (resid_f * lax.rsqrt(squares + 1e-06)[:, None] * norm_gain[None, :]).astype(
        jnp.bfloat16
    )
    rows = lax.all_gather(normed, "expert", axis=0, tiled=True)
    row_targets = lax.all_gather(targets, "expert", axis=0, tiled=True)
    logits = jnp.dot(rows, lm_weight, preferred_element_type=jnp.float32)
    fresh = shard_stats(logits, row_targets, base)
    top_all, total_all, chosen_all = tuple((new for new in fresh))
    top_got, total_got, chosen_got = (
        lax.all_to_all(top_all, "expert", split_axis=0, concat_axis=0, tiled=True),
        lax.all_to_all(total_all, "expert", split_axis=0, concat_axis=0, tiled=True),
        lax.all_to_all(chosen_all, "expert", split_axis=0, concat_axis=0, tiled=True),
    )
    top_got = top_got.reshape(expert_devs, tok_rows)
    total_got = total_got.reshape(expert_devs, tok_rows)
    chosen_got = chosen_got.reshape(expert_devs, tok_rows)
    best = jnp.max(top_got, axis=0)
    mass = jnp.sum(total_got * jnp.exp(top_got - best[None, :]), axis=0)
    chosen = jnp.sum(chosen_got, axis=0)
    best, mass, chosen = joined_all((best, mass, chosen), "vocab", join_stats)
    return chosen - best - jnp.log(mass)


def solution(mesh):
    in_specs = (
        P("expert", None),
        P("expert", None),
        P("expert", None),
        P("expert", None, "vocab"),
        P("expert", None, "vocab"),
        P("expert", "vocab", None),
        P(),
        P(None, ("expert", "vocab")),
        P("expert"),
    )
    out_specs = P("expert")
    return jax.shard_map(body, mesh=mesh, in_specs=in_specs, out_specs=out_specs, check_vma=False)
```

profile of v0, /device:TPU:0, one launch (start us, length us, event | category | flops | bytes accessed | tf_op | source)
XLA Modules:
  0.0 552.3 jit_solution(4479632245104566551)
XLA Ops:
  6.5 0.9 copy.47
  7.5 0.1 eq.52
  7.6 0.1 reshape.127
  7.8 1.8 reduce-window.6
  9.6 0.3 slice_reduce_fusion
  9.9 0.1 fusion.26
  10.0 0.1 reduce_sum.77
  10.2 0.1 copy.50
  10.2 0.7 compare_and_fusion
  10.9 0.8 fusion.4
  11.7 2.8 convolution_convert_fusion
  14.6 81.5 %all_to_all.52 = bf16[64,24,2048]{2,1,0:T(8,128)(2,1)S(1)} all-to-all(bf16[64,24,2048]{2,1,0:T(8,128)(2,1)S(1)} %bitcast.93), channel_id=1, replica_groups=mesh['expert'=32,'vocab'=4] {'expert'}, dimensions={0} | all-to-all | bytes 12582912 | tf_op jit(solution)/shard_map/all_to_all | solution.py:123
  96.1 2.6 copy-done.1
  98.7 4.9 fusion.2
  103.5 13.6 %convolution_bitcast_fusion = f32[32,2,24,2048]{3,2,0,1:T(8,128)} fusion(bf16[2,352,2048]{2,1,0:T(8,128)(2,1)} %param.14, f32[2,32,24,352]{3,2,1,0:T(8,128)} %fusion.2, bf16[2,2048,352]{1,2,0:T(8,128)(2,1)} %param.13, bf16[32,2,24,2048]{3,2,1,0:T(8,128)(2,1)} %bitcast.95), kind=kOutput, calls=%fused_computation.10 | convolution fusion | flops 4432429056 | bytes 26804224 | tf_op jit(solution)/shard_map/sltf,lfd->sltd/dot_general | solution.py:81
  117.1 2.2 slice-done
  119.3 2.2 copy.54
  121.5 4.9 all-to-all-start.1
  126.4 3.4 slice-done.1
  129.8 3.8 copy.55
  133.6 45.4 %all-to-all-done.1 = f32[32,2,8,2048]{3,2,1,0:T(8,128)} async-done(((f32[32,2,8,2048]{3,2,1,0:T(8,128)}), f32[32,2,8,2048]{3,2,1,0:T(8,128)}, u32[]{:S(2)}, u32[]{:S(2)}) %all-to-all-start.1) | async-done | bytes 4194336 | tf_op jit(solution)/shard_map/all_to_all | solution.py:29
  178.9 6.8 %all-to-all-start.2 = ((f32[32,2,16,2048]{3,2,1,0:T(8,128)}), f32[32,2,16,2048]{3,2,1,0:T(8,128)}, u32[]{:S(2)}, u32[]{:S(2)}) async-start(f32[32,2,16,2048]{3,2,1,0:T(8,128)} %copy.55), calls=%async_computation.2 | async-start | bytes 16777216 | tf_op jit(solution)/shard_map/all_to_all | solution.py:29
  185.8 0.1 copy.56
  186.0 0.1 mul.84
  186.1 0.1 copy.51
  186.2 0.1 copy.57
  186.4 112.9 %all-to-all-done.2 = f32[32,2,16,2048]{3,2,1,0:T(8,128)} async-done(((f32[32,2,16,2048]{3,2,1,0:T(8,128)}), f32[32,2,16,2048]{3,2,1,0:T(8,128)}, u32[]{:S(2)}, u32[]{:S(2)}) %all-to-all-start.2) | async-done | bytes 8388640 | tf_op jit(solution)/shard_map/all_to_all | solution.py:29
  299.3 11.3 %pad_maximum_fusion = f32[32,2,24,2048]{3,2,1,0:T(8,128)} fusion(f32[32,2,16,2048]{3,2,1,0:T(8,128)} %all-to-all-done.2, f32[32,2,8,2048]{3,2,1,0:T(8,128)} %all-to-all-done.1), kind=kLoop, calls=%fused_computation.1 | loop fusion | flops 3145728 | bytes 25165824 | tf_op jit(solution)/shard_map/concatenate | solution.py:30
  310.6 11.8 %gather_fusion = f32[768,2048]{1,0:T(8,128)} fusion(f32[1536,2048]{1,0:T(8,128)} %bitcast.92, s32[1024]{0:T(1024)S(1)} %pad_clamp_fusion), kind=kCustom, calls=%fused_computation | custom fusion | bytes 12585984 | tf_op jit(solution)/shard_map/jit(_take)/gather | solution.py:130
  322.4 7.8 %gather.7 = f32[128,6,2048]{2,1,0:T(8,128)} reshape(f32[768,2048]{1,0:T(8,128)} %gather_fusion) | data formatting | bytes 12582912 | tf_op jit(solution)/shard_map/jit(_take)/gather | solution.py:130
  330.3 6.5 %multiply_reduce_fusion = f32[128,2048]{1,0:T(8,128)S(1)} fusion(f32[128,6,2048]{2,1,0:T(8,128)} %gather.7, f32[128,6]{1,0:T(8,128)S(1)} %copy.57, pred[128,6]{1,0:T(8,128)(4,1)S(1)} %copy.51), kind=kLoop, calls=%fused_computation.4 | loop fusion | flops 4456448 | bytes 7343872 | tf_op jit(solution)/shard_map/reduce_sum | solution.py:133
  336.8 0.5 broadcast_in_dim.20
  337.3 47.0 %all_to_all.53 = f32[4,128,2048]{2,1,0:T(8,128)} all-to-all(f32[4,128,2048]{2,1,0:T(8,128)S(1)} %broadcast_in_dim.20), channel_id=1, replica_groups=mesh['expert'=32,'vocab'=4] {'vocab'}, dimensions={0} | all-to-all | bytes 8388608 | tf_op jit(solution)/shard_map/all_to_all | solution.py:35
  384.3 3.6 reduce_sum.80
  387.9 1.6 fusion.21
  389.5 2.3 fusion.23
  391.9 37.4 %all-gather = s32[32,1,128]{2,1,0:T(1,128)S(1)} all-gather(s32[1,1,128]{2,1,0:T(1,128)S(1)} %bitcast.109), channel_id=1, replica_groups=mesh['expert'=32,'vocab'=4] {'expert'}, dimensions={0}, use_global_device_ids=true | all-gather | bytes 16896 | tf_op jit(solution)/shard_map/all_gather | solution.py:143
  429.3 47.4 %all-gather.3.cloned.1.call-done = bf16[4096,2048]{1,0:T(8,128)(2,1)} async-done(((bf16[128,2048]{1,0:T(8,128)(2,1)}), bf16[4096,2048]{1,0:T(8,128)(2,1)}) %all-gather.3.cloned.1.call-update) | async-done | bytes 16777232 | tf_op jit(solution)/shard_map/all_gather | solution.py:142
  476.7 20.1 %fusion.33 = (f32[4096]{0:T(1024)}, f32[4096,768]{0,1:T(8,128)}) fusion(bf16[4096,2048]{1,0:T(8,128)(2,1)} %all-gather.3.cloned.1.call-done, bf16[2048,768]{1,0:T(8,128)(2,1)S(1)} %copy-done), kind=kOutput, calls=%fused_computation.55 | convolution fusion | flops 12888043520 | bytes 32522240 | tf_op jit(solution)/shard_map/dot_general | solution.py:144
  496.8 5.4 all-to-all-start.4
  502.2 7.2 %exponential_reduce_fusion = (f32[4096]{0:T(1024)}, f32[4096]{0:T(1024)}) fusion(f32[4096,768]{0,1:T(8,128)} %get-tuple-element.15, f32[4096]{0:T(1024)} %get-tuple-element.14, s32[4096]{0:T(1024)S(1)} %bitcast.97, s32[768]{0:T(1024)S(1)} %iota_add_fusion), kind=kLoop, calls=%fused_computation.3 | loop fusion | flops 15720448 | bytes 12651520 | tf_op jit(solution)/shard_map/reduce_sum | solution.py:88
  509.4 0.2 all-to-all-done.4
  509.6 7.2 %all-to-all-start.5 = ((f32[32,128,1]{1,2,0:T(1,128)}), f32[32,128,1]{1,2,0:T(1,128)S(1)}, u32[]{:S(2)}, u32[]{:S(2)}) async-start(f32[32,128,1]{1,2,0:T(1,128)} %bitcast.16), calls=%async_computation.5 | async-start | bytes 32768 | tf_op jit(solution)/shard_map/all_to_all | solution.py:149
  516.9 7.3 %all-to-all-done.5 = f32[32,128,1]{1,2,0:T(1,128)S(1)} async-done(((f32[32,128,1]{1,2,0:T(1,128)}), f32[32,128,1]{1,2,0:T(1,128)S(1)}, u32[]{:S(2)}, u32[]{:S(2)}) %all-to-all-start.5) | async-done | bytes 16416 | tf_op jit(solution)/shard_map/all_to_all | solution.py:149
  524.2 3.8 all-to-all-start.6
  528.0 7.3 %all-to-all-done.6 = f32[32,128,1]{1,2,0:T(1,128)S(1)} async-done(((f32[32,128,1]{1,2,0:T(1,128)}), f32[32,128,1]{1,2,0:T(1,128)S(1)}, u32[]{:S(2)}, u32[]{:S(2)}) %all-to-all-start.6) | async-done | bytes 16416 | tf_op jit(solution)/shard_map/all_to_all | solution.py:150
  535.4 9.4 %all_to_all.54 = f32[4,3,128]{2,1,0:T(4,128)S(1)} all-to-all(f32[4,3,128]{2,1,0:T(4,128)S(1)} %broadcast_in_dim.22), channel_id=1, replica_groups=mesh['expert'=32,'vocab'=4] {'vocab'}, dimensions={0} | all-to-all | bytes 12288 | tf_op jit(solution)/shard_map/all_to_all | solution.py:35
  545.0 0.5 subtract_bitcast_fusion
  (38 shorter events, 0.5 us)
Async XLA Ops:
  6.5 470.2 %copy-start = (bf16[2048,768]{1,0:T(8,128)(2,1)S(1)}, bf16[2048,768]{1,0:T(8,128)(2,1)}, u32[]{:S(2)}) copy-start(bf16[2048,768]{1,0:T(8,128)(2,1)} %param.16) | copy-start | bytes 9437188
  14.6 84.1 %copy-start.6 = (bf16[2,2048,352]{1,2,0:T(8,128)(2,1)S(1)}, bf16[2,2048,352]{1,2,0:T(8,128)(2,1)}, u32[]{:S(2)}) copy-start(bf16[2,2048,352]{1,2,0:T(8,128)(2,1)} %param.12) | copy-start | bytes 8650756
  96.1 2.6 copy-start.1
  117.1 2.2 slice-start
  121.5 57.4 %all-to-all-start.1 = ((f32[32,2,8,2048]{3,2,1,0:T(8,128)}), f32[32,2,8,2048]{3,2,1,0:T(8,128)}, u32[]{:S(2)}, u32[]{:S(2)}) async-start(f32[32,2,8,2048]{3,2,1,0:T(8,128)} %copy.54), calls=%async_computation.1 | async-start | bytes 8388608 | tf_op jit(solution)/shard_map/all_to_all | solution.py:29
  126.4 3.4 slice-start.1
  133.6 52.2 %copy-start.2 = (s32[128,6]{0,1:T(8,128)S(1)}, s32[128,6]{0,1:T(8,128)}, u32[]{:S(2)}) copy-start(s32[128,6]{0,1:T(8,128)} %param.10) | copy-start | bytes 9220
  133.6 52.7 %copy-start.4 = (f32[128,6]{0,1:T(8,128)S(1)}, f32[128,6]{0,1:T(8,128)}, u32[]{:S(2)}) copy-start(f32[128,6]{0,1:T(8,128)} %param.11) | copy-start | bytes 9220
  178.9 120.3 %all-to-all-start.2 = ((f32[32,2,16,2048]{3,2,1,0:T(8,128)}), f32[32,2,16,2048]{3,2,1,0:T(8,128)}, u32[]{:S(2)}, u32[]{:S(2)}) async-start(f32[32,2,16,2048]{3,2,1,0:T(8,128)} %copy.55), calls=%async_computation.2 | async-start | bytes 16777216 | tf_op jit(solution)/shard_map/all_to_all | solution.py:29
  185.8 290.9 %all-gather.3.cloned.1.call-start = ((), (), s32[]{:S(2)}) async-start(), calls=%async_computation.8 | async-start | bytes 17301504 | tf_op jit(solution)/shard_map/all_gather | solution.py:142
  337.3 52.2 %copy-start.3 = (f32[2048]{0:T(1024)S(1)}, f32[2048]{0:T(1024)}, u32[]{:S(2)}) copy-start(f32[2048]{0:T(1024)} %param.15) | copy-start | bytes 24580
  384.3 7.5 %copy-start.5 = (s32[128]{0:T(128)S(1)}, s32[128]{0:T(128)}, u32[]{:S(2)}) copy-start(s32[128]{0:T(128)} %param.17) | copy-start | bytes 1540
  496.8 12.8 %all-to-all-start.4 = ((f32[32,128,1]{1,2,0:T(1,128)}), f32[32,128,1]{1,2,0:T(1,128)S(1)}, u32[]{:S(2)}, u32[]{:S(2)}) async-start(f32[32,128,1]{1,2,0:T(1,128)} %bitcast.14), calls=%async_computation.4 | async-start | bytes 32768 | tf_op jit(solution)/shard_map/all_to_all | solution.py:148
  509.6 14.6 %all-to-all-start.5 = ((f32[32,128,1]{1,2,0:T(1,128)}), f32[32,128,1]{1,2,0:T(1,128)S(1)}, u32[]{:S(2)}, u32[]{:S(2)}) async-start(f32[32,128,1]{1,2,0:T(1,128)} %bitcast.16), calls=%async_computation.5 | async-start | bytes 32768 | tf_op jit(solution)/shard_map/all_to_all | solution.py:149
  524.2 11.2 %all-to-all-start.6 = ((f32[32,128,1]{1,2,0:T(1,128)}), f32[32,128,1]{1,2,0:T(1,128)S(1)}, u32[]{:S(2)}, u32[]{:S(2)}) async-start(f32[32,128,1]{1,2,0:T(1,128)} %bitcast.23), calls=%async_computation.6 | async-start | bytes 32768 | tf_op jit(solution)/shard_map/all_to_all | solution.py:150
Sparse Core Ops, SparseCore 0:
  392.0 84.6 all-gather.2
where the time goes:
time: 553 us; the launch traced here: 552 us
  waiting for transfers between devices  221 us (40%)
  blocking collectives  175 us (32%)
  matrix products  41.4 us (7%)
  local copies, waits for them, and re-layouts  36.7 us (7%)
  other arithmetic  36.7 us (7%)
  starting transfers between devices  28.1 us (5%)
  between operations  13.6 us (2%)
    all_to_all x2, waiting for transfers between devices, several_exchanges(): lax.all_to_all(share, axis, split_axis=0, concat_axis=0, tiled=True)  158 us
    all_to_all x1, blocking collectives, body(): lax.all_to_all(packed, 'expert', split_axis=0, concat_axis=0, tiled=True)  81.5 us
    all_to_all x2, blocking collectives, copy_for_each(): lax.all_to_all(jnp.broadcast_to(array[None], (count, *array.shape)), axis...  56.4 us
    all_gather x1, waiting for transfers between devices, body(): rows = lax.all_gather(normed, 'expert', axis=0, tiled=True)  47.4 us
    all_gather x1, blocking collectives, body(): row_targets = lax.all_gather(targets, 'expert', axis=0, tiled=True)  37.4 us
    dot_general x1, matrix products, body(): logits = jnp.dot(rows, lm_weight, preferred_element_type=jnp.float32)  20.1 us
    gather x2, local copies, waits for them, and re-layouts, body(): jnp.take(flat_back, target_rows.reshape(-1), axis=0)  19.6 us
    dot_general x1, matrix products, expert_rows(): jnp.einsum('sltf,lfd->sltd', hidden, w_down, preferred_element_type=jnp.f...  13.6 us
  transfers between devices with their start and end apart: 6, of which 6 were waited for; matrix products, arithmetic and copies ran while one was open for 2% of the time, Pallas kernels for 0%

commit v1 on v0

--- a/solution.py
+++ b/solution.py
@@ -140,7 +140,10 @@
         jnp.bfloat16
     )
     rows = lax.all_gather(normed, "expert", axis=0, tiled=True)
-    row_targets = lax.all_gather(targets, "expert", axis=0, tiled=True)
+    _connect_pools = lambda message, mesh_name: jnp.concatenate(
+        lax.all_to_all(jnp.stack([message] * lax.psum(1, mesh_name)), mesh_name, 0, 0), axis=0
+    )
+    row_targets = _connect_pools(targets, "expert")
     logits = jnp.dot(rows, lm_weight, preferred_element_type=jnp.float32)
     fresh = shard_stats(logits, row_targets, base)
     top_all, total_all, chosen_all = tuple((new for new in fresh))

time: 553 us -> 553 us (level)
  blocking collectives: 175 us -> 138 us
  starting transfers between devices: 28.1 us -> 48 us
  waiting for transfers between devices: 221 us -> 237 us
    all_gather x1 -> x0, blocking collectives: 37.4 us -> none  [body(): row_targets = lax.all_gather(targets, 'expert', axis=0, tiled=True)]
    all_to_all x0 -> x1, starting transfers between devices: none -> 19.9 us  [body(): lax.all_to_all(jnp.stack([message] * lax.psum(1, mesh_name)), mesh_name,...]
    all_gather x1, waiting for transfers between devices: 47.4 us -> 64.2 us  [body(): rows = lax.all_gather(normed, 'expert', axis=0, tiled=True)]
  transfers between devices with their start and end apart: 6 -> 7, of which waited for: 6 -> 6; matrix products, arithmetic and copies ran while one was open for 2% -> 6% of each run, Pallas kernels for 0% -> 0%
where the time goes in v1:
time: 553 us; the launch traced here: 552 us
  waiting for transfers between devices  237 us (43%)
  blocking collectives  138 us (25%)
  starting transfers between devices  48 us (9%)
  matrix products  41.4 us (7%)
  local copies, waits for them, and re-layouts  37.3 us (7%)
  other arithmetic  36.7 us (7%)
  between operations  13.6 us (2%)
    all_to_all x2, waiting for transfers between devices, several_exchanges(): lax.all_to_all(share, axis, split_axis=0, concat_axis=0, tiled=True)  158 us
    all_to_all x1, blocking collectives, body(): lax.all_to_all(packed, 'expert', split_axis=0, concat_axis=0, tiled=True)  81.5 us
    all_gather x1, waiting for transfers between devices, body(): rows = lax.all_gather(normed, 'expert', axis=0, tiled=True)  64.2 us
    all_to_all x2, blocking collectives, copy_for_each(): lax.all_to_all(jnp.broadcast_to(array[None], (count, *array.shape)), axis...  56.4 us
    dot_general x1, matrix products, body(): logits = jnp.dot(rows, lm_weight, preferred_element_type=jnp.float32)  20.1 us
    all_to_all x1, starting transfers between devices, body(): lax.all_to_all(jnp.stack([message] * lax.psum(1, mesh_name)), mesh_name,...  19.9 us
    gather x2, local copies, waits for them, and re-layouts, body(): jnp.take(flat_back, target_rows.reshape(-1), axis=0)  19.6 us
    dot_general x1, matrix products, expert_rows(): jnp.einsum('sltf,lfd->sltd', hidden, w_down, preferred_element_type=jnp.f...  13.6 us
  transfers between devices with their start and end apart: 7, of which 6 were waited for; matrix products, arithmetic and copies ran while one was open for 6% of the time, Pallas kernels for 0%

profile of v1, /device:TPU:0, one launch (start us, length us, event | category | flops | bytes accessed | tf_op | source)
XLA Modules:
  0.0 552.2 jit_solution(9565386547470136684)
XLA Ops:
  6.5 0.9 copy.47
  7.5 0.1 eq.54
  7.6 0.1 reshape.135
  7.8 1.8 reduce-window.6
  9.6 0.3 slice_reduce_fusion
  9.9 0.1 fusion.26
  10.0 0.1 reduce_sum.77
  10.2 0.7 compare_and_fusion
  10.9 0.8 fusion.4
  11.7 2.8 convolution_convert_fusion
  14.6 81.5 %all_to_all.58 = bf16[64,24,2048]{2,1,0:T(8,128)(2,1)S(1)} all-to-all(bf16[64,24,2048]{2,1,0:T(8,128)(2,1)S(1)} %bitcast.92), channel_id=1, replica_groups=mesh['expert'=32,'vocab'=4] {'expert'}, dimensions={0} | all-to-all | bytes 12582912 | tf_op jit(solution)/shard_map/all_to_all | solution.py:123
  96.1 2.6 copy-done.1
  98.7 4.9 fusion.2
  103.5 13.6 %convolution_bitcast_fusion = f32[32,2,24,2048]{3,2,0,1:T(8,128)} fusion(bf16[2,352,2048]{2,1,0:T(8,128)(2,1)} %param.14, f32[2,32,24,352]{3,2,1,0:T(8,128)} %fusion.2, bf16[2,2048,352]{1,2,0:T(8,128)(2,1)} %param.13, bf16[32,2,24,2048]{3,2,1,0:T(8,128)(2,1)} %bitcast.94), kind=kOutput, calls=%fused_computation.10 | convolution fusion | flops 4432429056 | bytes 26804224 | tf_op jit(solution)/shard_map/sltf,lfd->sltd/dot_general | solution.py:81
  117.1 2.2 slice-done
  119.3 2.2 copy.54
  121.5 4.9 all-to-all-start.1
  126.4 3.4 slice-done.1
  129.8 3.8 copy.55
  133.6 45.4 %all-to-all-done.1 = f32[32,2,8,2048]{3,2,1,0:T(8,128)} async-done(((f32[32,2,8,2048]{3,2,1,0:T(8,128)}), f32[32,2,8,2048]{3,2,1,0:T(8,128)}, u32[]{:S(2)}, u32[]{:S(2)}) %all-to-all-start.1) | async-done | bytes 4194336 | tf_op jit(solution)/shard_map/all_to_all | solution.py:29
  178.9 6.8 %all-to-all-start.2 = ((f32[32,2,16,2048]{3,2,1,0:T(8,128)}), f32[32,2,16,2048]{3,2,1,0:T(8,128)}, u32[]{:S(2)}, u32[]{:S(2)}) async-start(f32[32,2,16,2048]{3,2,1,0:T(8,128)} %copy.55), calls=%async_computation.2 | async-start | bytes 16777216 | tf_op jit(solution)/shard_map/all_to_all | solution.py:29
  185.8 0.1 copy.56
  186.0 0.1 mul.84
  186.1 0.1 copy.51
  186.2 0.1 copy.57
  186.4 112.9 %all-to-all-done.2 = f32[32,2,16,2048]{3,2,1,0:T(8,128)} async-done(((f32[32,2,16,2048]{3,2,1,0:T(8,128)}), f32[32,2,16,2048]{3,2,1,0:T(8,128)}, u32[]{:S(2)}, u32[]{:S(2)}) %all-to-all-start.2) | async-done | bytes 8388640 | tf_op jit(solution)/shard_map/all_to_all | solution.py:29
  299.3 11.3 %pad_maximum_fusion = f32[32,2,24,2048]{3,2,1,0:T(8,128)} fusion(f32[32,2,16,2048]{3,2,1,0:T(8,128)} %all-to-all-done.2, f32[32,2,8,2048]{3,2,1,0:T(8,128)} %all-to-all-done.1), kind=kLoop, calls=%fused_computation.1 | loop fusion | flops 3145728 | bytes 25165824 | tf_op jit(solution)/shard_map/concatenate | solution.py:30
  310.6 11.8 %gather_fusion = f32[768,2048]{1,0:T(8,128)} fusion(f32[1536,2048]{1,0:T(8,128)} %bitcast.91, s32[1024]{0:T(1024)S(1)} %pad_clamp_fusion), kind=kCustom, calls=%fused_computation | custom fusion | bytes 12585984 | tf_op jit(solution)/shard_map/jit(_take)/gather | solution.py:130
  322.4 7.8 %gather.7 = f32[128,6,2048]{2,1,0:T(8,128)} reshape(f32[768,2048]{1,0:T(8,128)} %gather_fusion) | data formatting | bytes 12582912 | tf_op jit(solution)/shard_map/jit(_take)/gather | solution.py:130
  330.3 6.5 %multiply_reduce_fusion = f32[128,2048]{1,0:T(8,128)S(1)} fusion(f32[128,6,2048]{2,1,0:T(8,128)} %gather.7, f32[128,6]{1,0:T(8,128)S(1)} %copy.57, pred[128,6]{1,0:T(8,128)(4,1)S(1)} %copy.51), kind=kLoop, calls=%fused_computation.4 | loop fusion | flops 4456448 | bytes 7343872 | tf_op jit(solution)/shard_map/reduce_sum | solution.py:133
  336.8 0.5 broadcast_in_dim.20
  337.3 47.0 %all_to_all.59 = f32[4,128,2048]{2,1,0:T(8,128)} all-to-all(f32[4,128,2048]{2,1,0:T(8,128)S(1)} %broadcast_in_dim.20), channel_id=1, replica_groups=mesh['expert'=32,'vocab'=4] {'vocab'}, dimensions={0} | all-to-all | bytes 8388608 | tf_op jit(solution)/shard_map/all_to_all | solution.py:35
  384.3 3.6 reduce_sum.80
  387.9 1.6 fusion.21
  389.5 2.3 fusion.23
  391.9 0.6 stack.2
  392.5 19.9 %all-to-all-start.6 = ((s32[32,1,128]{2,1,0:T(1,128)}), s32[32,1,128]{2,1,0:T(1,128)S(1)}, u32[]{:S(2)}, u32[]{:S(2)}) async-start(s32[32,1,128]{2,1,0:T(1,128)} %stack.2), calls=%async_computation.6 | async-start | bytes 32768 | tf_op jit(solution)/shard_map/all_to_all | solution.py:144
  412.4 64.2 %all-gather.2.cloned.1.call-done = bf16[4096,2048]{1,0:T(8,128)(2,1)} async-done(((bf16[128,2048]{1,0:T(8,128)(2,1)}), bf16[4096,2048]{1,0:T(8,128)(2,1)}) %all-gather.2.cloned.1.call-update) | async-done | bytes 16777232 | tf_op jit(solution)/shard_map/all_gather | solution.py:142
  476.6 20.1 %fusion.33 = (f32[4096]{0:T(1024)}, f32[4096,768]{0,1:T(8,128)}) fusion(bf16[4096,2048]{1,0:T(8,128)(2,1)} %all-gather.2.cloned.1.call-done, bf16[2048,768]{1,0:T(8,128)(2,1)S(1)} %copy-done), kind=kOutput, calls=%fused_computation.55 | convolution fusion | flops 12888043520 | bytes 32522240 | tf_op jit(solution)/shard_map/dot_general | solution.py:147
  496.7 5.4 all-to-all-start.4
  502.1 7.2 %exponential_reduce_fusion = (f32[4096]{0:T(1024)}, f32[4096]{0:T(1024)}) fusion(f32[4096,768]{0,1:T(8,128)} %get-tuple-element.15, f32[4096]{0:T(1024)} %get-tuple-element.14, s32[4096]{0:T(1024)S(1)} %bitcast.96, s32[768]{0:T(1024)S(1)} %iota_add_fusion), kind=kLoop, calls=%fused_computation.3 | loop fusion | flops 15720448 | bytes 12651520 | tf_op jit(solution)/shard_map/reduce_sum | solution.py:88
  509.3 0.2 all-to-all-done.4
  509.5 7.2 %all-to-all-start.5 = ((f32[32,128,1]{1,2,0:T(1,128)}), f32[32,128,1]{1,2,0:T(1,128)S(1)}, u32[]{:S(2)}, u32[]{:S(2)}) async-start(f32[32,128,1]{1,2,0:T(1,128)} %bitcast.16), calls=%async_computation.5 | async-start | bytes 32768 | tf_op jit(solution)/shard_map/all_to_all | solution.py:152
  516.7 7.3 %all-to-all-done.5 = f32[32,128,1]{1,2,0:T(1,128)S(1)} async-done(((f32[32,128,1]{1,2,0:T(1,128)}), f32[32,128,1]{1,2,0:T(1,128)S(1)}, u32[]{:S(2)}, u32[]{:S(2)}) %all-to-all-start.5) | async-done | bytes 16416 | tf_op jit(solution)/shard_map/all_to_all | solution.py:152
  524.1 3.8 all-to-all-start.7
  527.9 7.3 %all-to-all-done.7 = f32[32,128,1]{1,2,0:T(1,128)S(1)} async-done(((f32[32,128,1]{1,2,0:T(1,128)}), f32[32,128,1]{1,2,0:T(1,128)S(1)}, u32[]{:S(2)}, u32[]{:S(2)}) %all-to-all-start.7) | async-done | bytes 16416 | tf_op jit(solution)/shard_map/all_to_all | solution.py:153
  535.3 9.4 %all_to_all.60 = f32[4,3,128]{2,1,0:T(4,128)S(1)} all-to-all(f32[4,3,128]{2,1,0:T(4,128)S(1)} %broadcast_in_dim.22), channel_id=1, replica_groups=mesh['expert'=32,'vocab'=4] {'vocab'}, dimensions={0} | all-to-all | bytes 12288 | tf_op jit(solution)/shard_map/all_to_all | solution.py:35
  544.8 0.5 subtract_bitcast_fusion
  (40 shorter events, 0.5 us)
Async XLA Ops:
  6.5 470.0 %copy-start = (bf16[2048,768]{1,0:T(8,128)(2,1)S(1)}, bf16[2048,768]{1,0:T(8,128)(2,1)}, u32[]{:S(2)}) copy-start(bf16[2048,768]{1,0:T(8,128)(2,1)} %param.16) | copy-start | bytes 9437188
  14.6 84.1 %copy-start.6 = (bf16[2,2048,352]{1,2,0:T(8,128)(2,1)S(1)}, bf16[2,2048,352]{1,2,0:T(8,128)(2,1)}, u32[]{:S(2)}) copy-start(bf16[2,2048,352]{1,2,0:T(8,128)(2,1)} %param.12) | copy-start | bytes 8650756
  96.1 2.6 copy-start.1
  117.1 2.2 slice-start
  121.5 57.4 %all-to-all-start.1 = ((f32[32,2,8,2048]{3,2,1,0:T(8,128)}), f32[32,2,8,2048]{3,2,1,0:T(8,128)}, u32[]{:S(2)}, u32[]{:S(2)}) async-start(f32[32,2,8,2048]{3,2,1,0:T(8,128)} %copy.54), calls=%async_computation.1 | async-start | bytes 8388608 | tf_op jit(solution)/shard_map/all_to_all | solution.py:29
  126.4 3.4 slice-start.1
  133.6 52.2 %copy-start.2 = (s32[128,6]{0,1:T(8,128)S(1)}, s32[128,6]{0,1:T(8,128)}, u32[]{:S(2)}) copy-start(s32[128,6]{0,1:T(8,128)} %param.10) | copy-start | bytes 9220
  133.6 52.7 %copy-start.4 = (f32[128,6]{0,1:T(8,128)S(1)}, f32[128,6]{0,1:T(8,128)}, u32[]{:S(2)}) copy-start(f32[128,6]{0,1:T(8,128)} %param.11) | copy-start | bytes 9220
  178.9 120.3 %all-to-all-start.2 = ((f32[32,2,16,2048]{3,2,1,0:T(8,128)}), f32[32,2,16,2048]{3,2,1,0:T(8,128)}, u32[]{:S(2)}, u32[]{:S(2)}) async-start(f32[32,2,16,2048]{3,2,1,0:T(8,128)} %copy.55), calls=%async_computation.2 | async-start | bytes 16777216 | tf_op jit(solution)/shard_map/all_to_all | solution.py:29
  185.8 290.8 %all-gather.2.cloned.1.call-start = ((), (), s32[]{:S(2)}) async-start(), calls=%async_computation.9 | async-start | bytes 17301504 | tf_op jit(solution)/shard_map/all_gather | solution.py:142
  337.3 52.2 %copy-start.3 = (f32[2048]{0:T(1024)S(1)}, f32[2048]{0:T(1024)}, u32[]{:S(2)}) copy-start(f32[2048]{0:T(1024)} %param.15) | copy-start | bytes 24580
  384.3 7.5 %copy-start.5 = (s32[128]{0:T(128)S(1)}, s32[128]{0:T(128)}, u32[]{:S(2)}) copy-start(s32[128]{0:T(128)} %param.17) | copy-start | bytes 1540
  392.5 104.2 %all-to-all-start.6 = ((s32[32,1,128]{2,1,0:T(1,128)}), s32[32,1,128]{2,1,0:T(1,128)S(1)}, u32[]{:S(2)}, u32[]{:S(2)}) async-start(s32[32,1,128]{2,1,0:T(1,128)} %stack.2), calls=%async_computation.6 | async-start | bytes 32768 | tf_op jit(solution)/shard_map/all_to_all | solution.py:144
  496.7 12.8 %all-to-all-start.4 = ((f32[32,128,1]{1,2,0:T(1,128)}), f32[32,128,1]{1,2,0:T(1,128)S(1)}, u32[]{:S(2)}, u32[]{:S(2)}) async-start(f32[32,128,1]{1,2,0:T(1,128)} %bitcast.14), calls=%async_computation.4 | async-start | bytes 32768 | tf_op jit(solution)/shard_map/all_to_all | solution.py:151
  509.5 14.6 %all-to-all-start.5 = ((f32[32,128,1]{1,2,0:T(1,128)}), f32[32,128,1]{1,2,0:T(1,128)S(1)}, u32[]{:S(2)}, u32[]{:S(2)}) async-start(f32[32,128,1]{1,2,0:T(1,128)} %bitcast.16), calls=%async_computation.5 | async-start | bytes 32768 | tf_op jit(solution)/shard_map/all_to_all | solution.py:152
  524.1 11.2 %all-to-all-start.7 = ((f32[32,128,1]{1,2,0:T(1,128)}), f32[32,128,1]{1,2,0:T(1,128)S(1)}, u32[]{:S(2)}, u32[]{:S(2)}) async-start(f32[32,128,1]{1,2,0:T(1,128)} %bitcast.22), calls=%async_computation.7 | async-start | bytes 32768 | tf_op jit(solution)/shard_map/all_to_all | solution.py:153
Sparse Core Ops, SparseCore 0:
  392.0 84.5 all-gather.1
